TPU v7x, 256 devices: a whole 4x4x8 slice. The times are simulated.
256 devices in a mesh: blk: 64 (over y, z, core), pair: 4 (over x).
Axes of the slice: x: 4, y: 4, z: 8, core: 2. Of those that a mesh axis runs over, the one named last changes fastest.
Arguments:
- raw_strain: bfloat16 [4, 9216, 8192], P('pair', 'blk'), may hold values from -6 to 6
- aa_taps: bfloat16 [64], replicated, may hold values from -0.75 to 0.75
- white_taps: bfloat16 [255], replicated, may hold values from -0.375 to 0.375
- src_channels: int32 [64, 64], replicated, may hold values from 0 to 8191, as said below
- recv_lo: int32 [64, 64], P('blk'), may hold values from 0 to 63
- recv_hi: int32 [64, 64], P('blk'), may hold values from 65 to 128
Outputs:
- xcorr: float32 [64, 1024, 64, 128], P('blk', 'pair')
Inputs may be any that keep to these rules, and one draw needn't show every extreme that they name: `src_channels`: row b lists 64 distinct channels: exactly 2 channels from each of 32 distinct tiles and none from the other tiles; tile of channel c is c // 128.
All inputs are finite; a program needn't handle non-finite values.
Results may differ from a plain program's by a relative error of at most 0.0052.
Values may be sent and summed in bfloat16 or wider, within the bound.
A program may use at most 128 MiB of HBM per device.

v0:
```python
import math
import jax
import jax.numpy as jnp
from jax import lax
from jax.sharding import PartitionSpec as P

DECIM = 8
KA = 64
LAGS = 1024
CAP = 2


def extended_2(cells, sides, width):
    for axis, dim in sides:
        count = lax.axis_size(axis)
        ends = count - 1
        head = lax.slice_in_dim(cells, 0, width, axis=dim)
        tail = lax.slice_in_dim(cells, cells.shape[dim] - width, cells.shape[dim], axis=dim)
        cells = jnp.concatenate(
            [
                lax.ppermute(tail, axis, [(i, (i + 1) % count) for i in range(ends)]),
                cells,
                lax.ppermute(head, axis, [((i + 1) % count, i) for i in range(ends)]),
            ],
            axis=dim,
        )
    return cells


def whiten_matrix(white_taps, length):
    n_taps = white_taps.shape[0]
    half = n_taps // 2
    left = length - 1 - half
    right = 2 * length - 1 - left - n_taps
    spread = jnp.pad(white_taps, (left, right))
    rolled = jnp.roll(spread, length)
    tiled = jnp.tile(rolled, length)[: length * (2 * length - 2)]
    return tiled.reshape(length, 2 * length - 2)[:, :length]


def body(raw_strain, aa_taps, white_taps, src_channels, recv_lo, recv_hi):
    raw_len = raw_strain.shape[1]
    short_len = raw_len // DECIM
    channels = raw_strain.shape[2]
    n_blocks = lax.axis_size("blk")
    tile = channels // n_blocks
    seg_len = short_len * n_blocks
    span = seg_len - LAGS
    extended = extended_2(raw_strain[0], (("blk", 0),), KA // 2)
    out_rows = jnp.arange(short_len)[:, None]
    in_cols = jnp.arange(raw_len + KA)[None, :]
    offset = in_cols - DECIM * out_rows
    valid = (offset >= 0) & (offset < KA)
    aa_matrix = jnp.where(valid, aa_taps[jnp.clip(offset, 0, KA - 1)], jnp.zeros((), aa_taps.dtype))
    decimated = jnp.dot(aa_matrix, extended, preferred_element_type=jnp.float32).astype(
        jnp.bfloat16
    )
    white_matrix = whiten_matrix(white_taps, seg_len)
    n_src = src_channels.shape[1]
    n_tiles = src_channels.shape[0]
    tile_raw = lax.all_to_all(decimated, "blk", split_axis=1, concat_axis=0, tiled=True)
    white_tile = jnp.dot(white_matrix, tile_raw, preferred_element_type=jnp.float32).astype(
        jnp.bfloat16
    )
    tile_of = src_channels // tile
    chan_of = src_channels - tile_of * tile
    same = tile_of[:, :, None] == tile_of[:, None, :]
    earlier = jnp.arange(n_src)[None, :] < jnp.arange(n_src)[:, None]
    slot_of = jnp.sum((same & earlier[None]).astype(jnp.int32), axis=2)
    mine = lax.axis_index("blk")
    belongs = tile_of == mine
    one_slot = (slot_of[:, :, None] == jnp.arange(CAP)[None, None, :]) & belongs[:, :, None]
    one_chan = chan_of[:, :, None] == jnp.arange(tile)[None, None, :]
    picker = jnp.einsum(
        "dkc,dkr->dcr",
        one_slot.astype(jnp.bfloat16),
        one_chan.astype(jnp.bfloat16),
        preferred_element_type=jnp.float32,
    ).astype(jnp.bfloat16)
    outgoing = jnp.einsum(
        "dcr,tr->dct", picker, white_tile, preferred_element_type=jnp.float32
    ).astype(jnp.bfloat16)
    incoming = lax.all_to_all(outgoing, "blk", split_axis=0, concat_axis=0, tiled=True)
    own_tiles = lax.dynamic_index_in_dim(tile_of, mine, 0, keepdims=False)
    own_slots = lax.dynamic_index_in_dim(slot_of, mine, 0, keepdims=False)
    selector = (own_tiles[:, None, None] == jnp.arange(n_tiles)[None, :, None]) & (
        own_slots[:, None, None] == jnp.arange(CAP)[None, None, :]
    )
    sources = jnp.einsum(
        "kec,ect->tk", selector.astype(jnp.bfloat16), incoming, preferred_element_type=jnp.float32
    ).astype(jnp.bfloat16)
    source_window = sources[LAGS // 2 : LAGS // 2 + span]
    lag_share = LAGS // lax.axis_size("pair")
    lag_start = lax.axis_index("pair") * lag_share
    lag_block = math.gcd(128, lag_share)
    n_lag_blocks = lag_share // lag_block
    initial = jnp.zeros((lag_share, n_src, tile), jnp.float32)
    total = initial
    tiles_in = lax.all_gather(white_tile[None], "pair", axis=0, tiled=True)
    sources_in = lax.all_gather(source_window[None], "pair", axis=0, tiled=True)
    for segment in range(tiles_in.shape[0]):
        window = lax.dynamic_slice_in_dim(tiles_in[segment], lag_start, span + lag_share, 0)
        parts = []
        for block in range(n_lag_blocks):
            base = block * lag_block
            hankel = jnp.stack(
                [window[base + shift : base + shift + span] for shift in range(lag_block)], 1
            )
            parts.append(
                jnp.einsum(
                    "tk,tjr->jkr", sources_in[segment], hankel, preferred_element_type=jnp.float32
                )
            )
        total = total + jnp.concatenate(parts, 0)
    scale = 1.0 / math.sqrt(span * lax.axis_size("pair"))
    position = jnp.arange(tile)[None, :]
    inside = (position >= recv_lo[0][:, None]) & (position < recv_hi[0][:, None])
    mask = jnp.where(inside, jnp.float32(scale), jnp.float32(0.0))
    return (total * mask[None])[None]


def solution(mesh):
    placed = (P("pair", "blk", None), P(), P(), P(), P("blk", None), P("blk", None))
    return jax.shard_map(
        body, mesh=mesh, in_specs=placed, out_specs=P("blk", "pair", None, None), check_vma=False
    )
```

profile of v0, /device:TPU:2, one launch (start us, length us, event | category | flops | bytes accessed | tf_op | source)
XLA Modules:
  0.0 203.3 jit_solution(10262311969563306636)
XLA Ops:
  6.5 0.0 copy-start
  6.5 1.3 slice_bitcast_fusion.1
  7.8 1.8 collective-permute-start
  9.6 1.3 collective-permute-start.1
  10.9 0.1 compare_select_fusion
  11.0 0.1 reshape.2337
  11.1 21.4 %gather_fusion = bf16[3744]{0:T(1024)(128)(2,1)S(1)} fusion(bf16[64]{0:T(256)(128)(2,1)S(1)} %copy-done, s32[4096]{0:T(1024)S(1)} %pad_clamp_fusion), kind=kCustom, calls=%fused_computation | custom fusion | bytes 29952 | tf_op jit(solution)/shard_map/gather | solution.py:54
  32.5 0.1 reshape.2336
  32.6 0.0 collective-permute-done
  32.6 0.0 collective-permute-done.1
  32.6 0.0 copy-start.3
  32.6 2.3 %convolution_convert_fusion = bf16[18,8192]{1,0:T(8,128)(2,1)S(1)} fusion(bf16[32,8192]{1,0:T(8,128)(2,1)S(1)} %collective-permute-done.1, bf16[144,8192]{1,0:T(8,128)(2,1)} %bitcast.4185, bf16[32,8192]{1,0:T(8,128)(2,1)S(1)} %collective-permute-done, bf16[18,208]{1,0:T(8,128)(2,1)S(1)} %reshape.2336, s32[18]{0:T(128)S(1)} %iota_multiply_fusion), kind=kOutput, calls=%fused_computation.1 | convolution fusion | flops 71731488 | bytes 3710344 | tf_op jit(solution)/shard_map/dot_general | solution.py:55
  34.9 0.1 copy.16
  35.0 1.0 copy.12
  36.0 15.8 %all-to-all-start = ((bf16[18,64,128]{2,0,1:T(8,128)(2,1)}), bf16[18,64,128]{2,0,1:T(8,128)(2,1)S(1)}, u32[]{:S(2)}, u32[]{:S(2)}) async-start(bf16[18,64,128]{2,0,1:T(8,128)(2,1)} %copy.12), calls=%async_computation | async-start | bytes 786432 | tf_op jit(solution)/shard_map/all_to_all | solution.py:61
  51.8 0.6 all-gather.4.cloned.1.call-start
  52.4 0.1 pad_slice_fusion.1
  52.5 2.7 %tile.4 = bf16[1152,2303]{1,0:T(8,128)(2,1)} broadcast(bf16[2303]{0:T(1024)(128)(2,1)S(1)} %pad_maximum_fusion), dimensions={1} | broadcast | bytes 5310718 | tf_op jit(solution)/shard_map/tile | solution.py:37
  55.2 14.8 %tile.10 = bf16[2653056]{0:T(1024)(128)(2,1)} reshape(bf16[1152,2303]{1,0:T(8,128)(2,1)} %tile.4) | data formatting | bytes 10612224 | tf_op jit(solution)/shard_map/tile | solution.py:37
  70.0 5.8 %slice.5204 = bf16[2651904]{0:T(1024)(128)(2,1)} slice(bf16[2653056]{0:T(1024)(128)(2,1)} %tile.10), slice={[0:2651904]} | slice | bytes 10607616 | tf_op jit(solution)/shard_map/slice | solution.py:37
  75.8 13.2 %reshape.2334 = bf16[1152,2302]{1,0:T(8,128)(2,1)} reshape(bf16[2651904]{0:T(1024)(128)(2,1)} %slice.5204) | data formatting | bytes 10607616 | tf_op jit(solution)/shard_map/reshape | solution.py:38
  89.0 0.0 all-to-all-done
  89.0 0.1 all_to_all.20
  89.1 3.3 %fusion.10 = bf16[1152,128]{1,0:T(8,128)(2,1)} fusion(bf16[1152,128]{1,0:T(8,128)(2,1)S(1)} %all_to_all.20, bf16[1152,2302]{1,0:T(8,128)(2,1)} %reshape.2334), kind=kOutput, calls=%fused_computation.13 | convolution fusion | flops 339886080 | bytes 3244032 | tf_op jit(solution)/shard_map/dot_general | solution.py:62
  92.5 0.0 all-gather.4.cloned.1.call-update
  92.5 1.9 convert_reduce_fusion
  94.4 0.9 fusion.14
  95.3 1.2 convolution_convert_fusion.1
  96.6 1.0 copy.14
  97.6 10.3 %all-to-all-start.1 = ((bf16[64,2,1152]{2,1,0:T(2,128)(2,1)}), bf16[64,2,1152]{2,1,0:T(2,128)(2,1)S(1)}, u32[]{:S(2)}, u32[]{:S(2)}) async-start(bf16[64,2,1152]{2,1,0:T(2,128)(2,1)} %copy.14), calls=%async_computation.1 | async-start | bytes 589824 | tf_op jit(solution)/shard_map/all_to_all | solution.py:83
  107.9 0.1 iota_compare_fusion.6
  108.0 0.0 copy-done.5
  108.0 0.1 fusion.26
  108.1 12.4 %all-to-all-done.1 = bf16[64,2,1152]{2,1,0:T(2,128)(2,1)S(1)} async-done(((bf16[64,2,1152]{2,1,0:T(2,128)(2,1)}), bf16[64,2,1152]{2,1,0:T(2,128)(2,1)S(1)}, u32[]{:S(2)}, u32[]{:S(2)}) %all-to-all-start.1) | async-done | bytes 294944 | tf_op jit(solution)/shard_map/all_to_all | solution.py:83
  120.5 0.3 convolution_bitcast_fusion
  120.8 11.2 %all-gather.1 = bf16[512,64]{0,1:T(8,128)(2,1)S(1)} all-gather(bf16[128,64]{0,1:T(8,128)(2,1)S(1)} %slice.9333), channel_id=3, replica_groups=mesh['blk'=64,'pair'=4] {'pair'}, dimensions={0}, use_global_device_ids=true | all-gather | bytes 81920 | tf_op jit(solution)/shard_map/all_gather | solution.py:100
  132.0 1.3 fusion.44
  139.6 2.7 %convolution_bitcast_fusion.1 = f32[1,128,64,128]{3,2,1,0:T(8,128)} fusion(bf16[128,128,128]{2,0,1:T(8,128)(2,1)S(1)} %constant_dynamic-update-slice_fusion.896, bf16[512,64]{0,1:T(8,128)(2,1)S(1)} %all-gather.1), kind=kOutput, calls=%fused_computation.16 | convolution fusion | flops 268435456 | bytes 8404992 | tf_op jit(solution)/shard_map/tk,tjr->jkr/dot_general | solution.py:110
  142.3 2.6 %convolution_bitcast_fusion.2 = f32[1,128,64,128]{3,2,1,0:T(8,128)} fusion(bf16[128,128,128]{2,0,1:T(8,128)(2,1)S(1)} %constant_dynamic-update-slice_fusion.768, bf16[512,64]{0,1:T(8,128)(2,1)S(1)} %all-gather.1), kind=kOutput, calls=%fused_computation.17 | convolution fusion | flops 268435456 | bytes 8404992 | tf_op jit(solution)/shard_map/tk,tjr->jkr/dot_general | solution.py:110
  148.0 2.7 %convolution_bitcast_fusion.3 = f32[1,128,64,128]{3,2,1,0:T(8,128)} fusion(bf16[128,128,128]{2,0,1:T(8,128)(2,1)S(1)} %constant_dynamic-update-slice_fusion.640, bf16[512,64]{0,1:T(8,128)(2,1)S(1)} %all-gather.1), kind=kOutput, calls=%fused_computation.18 | convolution fusion | flops 268435456 | bytes 8404992 | tf_op jit(solution)/shard_map/tk,tjr->jkr/dot_general | solution.py:110
  153.2 0.4 constant_dynamic-update-slice_fusion.532
  154.1 2.7 %convolution_bitcast_fusion.4 = f32[1,128,64,128]{3,2,1,0:T(8,128)} fusion(bf16[128,128,128]{2,0,1:T(8,128)(2,1)S(1)} %constant_dynamic-update-slice_fusion.512, bf16[512,64]{0,1:T(8,128)(2,1)S(1)} %all-gather.1), kind=kOutput, calls=%fused_computation.19 | convolution fusion | flops 268435456 | bytes 8404992 | tf_op jit(solution)/shard_map/tk,tjr->jkr/dot_general | solution.py:110
  159.8 2.7 %convolution_bitcast_fusion.5 = f32[1,128,64,128]{3,2,1,0:T(8,128)} fusion(bf16[128,128,128]{2,0,1:T(8,128)(2,1)S(1)} %constant_dynamic-update-slice_fusion.384, bf16[512,64]{0,1:T(8,128)(2,1)S(1)} %all-gather.1), kind=kOutput, calls=%fused_computation.20 | convolution fusion | flops 268435456 | bytes 8404992 | tf_op jit(solution)/shard_map/tk,tjr->jkr/dot_general | solution.py:110
  165.6 2.6 %convolution_bitcast_fusion.6 = f32[1,128,64,128]{3,2,1,0:T(8,128)} fusion(bf16[128,128,128]{2,0,1:T(8,128)(2,1)S(1)} %constant_dynamic-update-slice_fusion.256, bf16[512,64]{0,1:T(8,128)(2,1)S(1)} %all-gather.1), kind=kOutput, calls=%fused_computation.21 | convolution fusion | flops 268435456 | bytes 8404992 | tf_op jit(solution)/shard_map/tk,tjr->jkr/dot_general | solution.py:110
  171.2 2.7 %convolution_bitcast_fusion.7 = f32[1,128,64,128]{3,2,1,0:T(8,128)} fusion(bf16[128,128,128]{2,0,1:T(8,128)(2,1)S(1)} %constant_dynamic-update-slice_fusion.128, bf16[512,64]{0,1:T(8,128)(2,1)S(1)} %all-gather.1), kind=kOutput, calls=%fused_computation.22 | convolution fusion | flops 268435456 | bytes 8404992 | tf_op jit(solution)/shard_map/tk,tjr->jkr/dot_general | solution.py:110
  175.5 0.2 constant_dynamic-update-slice_fusion.60
  177.1 2.7 %convolution_bitcast_fusion.8 = f32[1,128,64,128]{3,2,1,0:T(8,128)} fusion(bf16[128,128,128]{2,0,1:T(8,128)(2,1)S(1)} %constant_dynamic-update-slice_fusion, bf16[512,64]{0,1:T(8,128)(2,1)S(1)} %all-gather.1), kind=kOutput, calls=%fused_computation.23 | convolution fusion | flops 268435456 | bytes 8404992 | tf_op jit(solution)/shard_map/tk,tjr->jkr/dot_general | solution.py:110
  179.8 16.4 %fusion.2 = f32[1,256,64,128]{3,2,1,0:T(8,128)} fusion(f32[1,128,64,128]{3,2,1,0:T(8,128)} %convolution_bitcast_fusion.7, f32[1,128,64,128]{3,2,1,0:T(8,128)} %convolution_bitcast_fusion.8, f32[1,128,64,128]{3,2,1,0:T(8,128)} %convolution_bitcast_fusion.5, f32[1,128,64,128]{3,2,1,0:T(8,128)} %convolution_bitcast_fusion.6, ...), kind=kLoop, calls=%fused_computation.5 | loop fusion | flops 16777216 | bytes 41975808 | tf_op jit(solution)/shard_map/mul | solution.py:119
  (1045 shorter events, 20.3 us)
Async XLA Ops:
  6.5 4.6 %copy-start = (bf16[64]{0:T(256)(128)(2,1)S(1)}, bf16[64]{0:T(256)(128)(2,1)}, u32[]{:S(2)}) copy-start(bf16[64]{0:T(256)(128)(2,1)} %param.7) | copy-start | bytes 388
  7.8 24.7 %collective-permute-start = (bf16[32,8192]{1,0:T(8,128)(2,1)S(1)}, bf16[32,8192]{1,0:T(8,128)(2,1)S(1)}, u32[]{:S(2)}, u32[]{:S(2)}) collective-permute-start(bf16[32,8192]{1,0:T(8,128)(2,1)S(1)} %get-tuple-element.5), channel_id=1, source_target_pairs={{0,4},{4,8},{8,12},{12,16},{16,20},{20,24},{24,28},{28,32},{32,36}... | collective-permute-start | bytes 1572872 | tf_op jit(solution)/shard_map/ppermute | solution.py:21
  9.6 23.0 %collective-permute-start.1 = (bf16[32,8192]{1,0:T(8,128)(2,1)S(1)}, bf16[32,8192]{1,0:T(8,128)(2,1)S(1)}, u32[]{:S(2)}, u32[]{:S(2)}) collective-permute-start(bf16[32,8192]{1,0:T(8,128)(2,1)S(1)} %get-tuple-element.6), channel_id=1, source_target_pairs={{4,0},{8,4},{12,8},{16,12},{20,16},{24,20},{28,24},{32,28},{36,32}... | collective-permute-start | bytes 1572872 | tf_op jit(solution)/shard_map/ppermute | solution.py:23
  32.6 19.8 %copy-start.3 = (bf16[255]{0:T(256)(128)(2,1)S(1)}, bf16[255]{0:T(256)(128)(2,1)}, u32[]{:S(2)}) copy-start(bf16[255]{0:T(256)(128)(2,1)} %param.8) | copy-start | bytes 1534
  36.0 53.0 %all-to-all-start = ((bf16[18,64,128]{2,0,1:T(8,128)(2,1)}), bf16[18,64,128]{2,0,1:T(8,128)(2,1)S(1)}, u32[]{:S(2)}, u32[]{:S(2)}) async-start(bf16[18,64,128]{2,0,1:T(8,128)(2,1)} %copy.12), calls=%async_computation | async-start | bytes 786432 | tf_op jit(solution)/shard_map/all_to_all | solution.py:61
  51.8 80.2 %all-gather.4.cloned.1.call-start = ((), (), s32[]{:S(2)}) async-start(), calls=%async_computation.2 | async-start | bytes 1474560 | tf_op jit(solution)/shard_map/all_gather | solution.py:99
  75.8 13.2 %copy-start.2 = (s32[64,64]{1,0:T(8,128)S(1)}, s32[64,64]{1,0:T(8,128)}, u32[]{:S(2)}) copy-start(s32[64,64]{1,0:T(8,128)} %param.9) | copy-start | bytes 49156
  88.9 19.0 %copy-start.4 = (s32[1,64]{1,0:T(1,128)S(1)}, s32[1,64]{1,0:T(1,128)}, u32[]{:S(2)}) copy-start(s32[1,64]{1,0:T(1,128)} %param.11) | copy-start | bytes 772
  88.9 19.1 %copy-start.5 = (s32[1,64]{1,0:T(1,128)S(1)}, s32[1,64]{1,0:T(1,128)}, u32[]{:S(2)}) copy-start(s32[1,64]{1,0:T(1,128)} %param.10) | copy-start | bytes 772
  97.6 22.9 %all-to-all-start.1 = ((bf16[64,2,1152]{2,1,0:T(2,128)(2,1)}), bf16[64,2,1152]{2,1,0:T(2,128)(2,1)S(1)}, u32[]{:S(2)}, u32[]{:S(2)}) async-start(bf16[64,2,1152]{2,1,0:T(2,128)(2,1)} %copy.14), calls=%async_computation.1 | async-start | bytes 589824 | tf_op jit(solution)/shard_map/all_to_all | solution.py:83
  179.8 16.4 %copy-start.1 = (bf16[64]{0:T(256)(128)(2,1)S(1)}, bf16[64]{0:T(256)(128)(2,1)}, u32[]{:S(2)}) copy-start(bf16[64]{0:T(256)(128)(2,1)} %param.7) | copy-start | bytes 388
Sparse Core Ops, SparseCore 0:
  92.6 27.0 all-gather.3
where the time goes:
time: 206 us; the launch traced here: 203 us
  local copies, waits for them, and re-layouts  83.7 us (41%)
  starting transfers between devices  29.8 us (14%)
  matrix products  29.4 us (14%)
  other arithmetic  18.6 us (9%)
  between operations  18.3 us (9%)
  waiting for transfers between devices  12.4 us (6%)
  blocking collectives  11.2 us (5%)
    gather x2, local copies, waits for them, and re-layouts, body(): aa_taps[jnp.clip(offset, 0, KA - 1)]  21.5 us
    dot_general x8, matrix products, body(): jnp.einsum('tk,tjr->jkr', sources_in[segment], hankel, preferred_element_...  21.4 us
    unnamed x1029, local copies, waits for them, and re-layouts  20.7 us
    another operation x2, local copies, waits for them, and re-layouts, whiten_matrix(): tiled = jnp.tile(rolled, length)[:length * (2 * length - 2)]  17.5 us
    mul x1, other arithmetic, body(): return (total * mask[None])[None]  16.4 us
    all_to_all x1, starting transfers between devices, body(): lax.all_to_all(decimated, 'blk', split_axis=1, concat_axis=0, tiled=True)  15.8 us
    reshape x1, local copies, waits for them, and re-layouts, whiten_matrix(): return tiled.reshape(length, 2 * length - 2)[:, :length]  13.2 us
    all_to_all x1, waiting for transfers between devices, body(): lax.all_to_all(outgoing, 'blk', split_axis=0, concat_axis=0, tiled=True)  12.4 us
  transfers between devices with their start and end apart: 5, of which 1 were waited for; matrix products, arithmetic and copies ran while one was open for 31% of the time, Pallas kernels for 0%

commit v1 on v0

--- a/solution.py
+++ b/solution.py
@@ -97,7 +97,10 @@
     initial = jnp.zeros((lag_share, n_src, tile), jnp.float32)
     total = initial
     tiles_in = lax.all_gather(white_tile[None], "pair", axis=0, tiled=True)
-    sources_in = lax.all_gather(source_window[None], "pair", axis=0, tiled=True)
+    sources_in = jnp.concatenate(
+        lax.all_to_all(jnp.stack([source_window[None]] * lax.axis_size("pair")), "pair", 0, 0),
+        axis=0,
+    )
     for segment in range(tiles_in.shape[0]):
         window = lax.dynamic_slice_in_dim(tiles_in[segment], lag_start, span + lag_share, 0)
         parts = []

time: 206 us -> 365 us (1.77)
  local copies, waits for them, and re-layouts: 83.7 us -> 241 us
  blocking collectives: 11.2 us -> 0 us
  matrix products: 29.4 us -> 36.7 us
  starting transfers between devices: 29.8 us -> 34.8 us
    unnamed x1029 -> x1051, local copies, waits for them, and re-layouts: 20.7 us -> 176 us
    all_gather x1 -> x0, blocking collectives: 11.2 us -> none  [body(): sources_in = lax.all_gather(source_window[None], 'pair', axis=0, tiled=True)]
    dot_general x8, matrix products: 21.4 us -> 28.7 us  [body(): jnp.einsum('tk,tjr->jkr', sources_in[segment], hankel, preferred_element_...]
    all_to_all x0 -> x1, starting transfers between devices: none -> 5.01 us  [body(): lax.all_to_all(jnp.stack([source_window[None]] * lax.axis_size('pair')),...]
  transfers between devices with their start and end apart: 5 -> 6, of which waited for: 1 -> 1; matrix products, arithmetic and copies ran while one was open for 31% -> 67% of each run, Pallas kernels for 0% -> 0%
where the time goes in v1:
time: 365 us; the launch traced here: 361 us
  local copies, waits for them, and re-layouts  241 us (66%)
  matrix products  36.7 us (10%)
  starting transfers between devices  34.8 us (10%)
  other arithmetic  18.6 us (5%)
  between operations  17.4 us (5%)
  waiting for transfers between devices  12.4 us (3%)
    unnamed x1051, local copies, waits for them, and re-layouts  176 us
    dot_general x8, matrix products, body(): jnp.einsum('tk,tjr->jkr', sources_in[segment], hankel, preferred_element_...  28.7 us
    gather x2, local copies, waits for them, and re-layouts, body(): aa_taps[jnp.clip(offset, 0, KA - 1)]  21.5 us
    another operation x2, local copies, waits for them, and re-layouts, whiten_matrix(): tiled = jnp.tile(rolled, length)[:length * (2 * length - 2)]  17.6 us
    mul x1, other arithmetic, body(): return (total * mask[None])[None]  16.4 us
    all_to_all x1, starting transfers between devices, body(): lax.all_to_all(decimated, 'blk', split_axis=1, concat_axis=0, tiled=True)  15.8 us
    reshape x1, local copies, waits for them, and re-layouts, whiten_matrix(): return tiled.reshape(length, 2 * length - 2)[:, :length]  13.2 us
    all_to_all x1, waiting for transfers between devices, body(): lax.all_to_all(outgoing, 'blk', split_axis=0, concat_axis=0, tiled=True)  12.4 us
  transfers between devices with their start and end apart: 6, of which 1 were waited for; matrix products, arithmetic and copies ran while one was open for 67% of the time, Pallas kernels for 0%

profile of v1, /device:TPU:2, one launch (start us, length us, event | category | flops | bytes accessed | tf_op | source)
XLA Modules:
  0.0 361.1 jit_solution(4460731010223978534)
XLA Ops:
  6.5 1.3 slice_bitcast_fusion.1
  7.8 1.8 collective-permute-start
  9.6 1.3 collective-permute-start.1
  11.1 21.4 %gather_fusion = bf16[3744]{0:T(1024)(128)(2,1)S(1)} fusion(bf16[64]{0:T(256)(128)(2,1)S(1)} %copy-done, s32[4096]{0:T(1024)S(1)} %pad_clamp_fusion), kind=kCustom, calls=%fused_computation | custom fusion | bytes 29952 | tf_op jit(solution)/shard_map/gather | solution.py:54
  32.6 2.3 convolution_convert_fusion
  35.0 1.0 copy.12
  36.0 15.8 %all-to-all-start = ((bf16[18,64,128]{2,0,1:T(8,128)(2,1)}), bf16[18,64,128]{2,0,1:T(8,128)(2,1)S(1)}, u32[]{:S(2)}, u32[]{:S(2)}) async-start(bf16[18,64,128]{2,0,1:T(8,128)(2,1)} %copy.12), calls=%async_computation | async-start | bytes 786432 | tf_op jit(solution)/shard_map/all_to_all | solution.py:61
  52.5 2.7 tile.4
  55.2 14.8 %tile.10 = bf16[2653056]{0:T(1024)(128)(2,1)} reshape(bf16[1152,2303]{1,0:T(8,128)(2,1)} %tile.4) | data formatting | bytes 10612224 | tf_op jit(solution)/shard_map/tile | solution.py:37
  70.0 5.8 %slice.5204 = bf16[2651904]{0:T(1024)(128)(2,1)} slice(bf16[2653056]{0:T(1024)(128)(2,1)} %tile.10), slice={[0:2651904]} | slice | bytes 10607616 | tf_op jit(solution)/shard_map/slice | solution.py:37
  75.8 13.2 %reshape.2345 = bf16[1152,2302]{1,0:T(8,128)(2,1)} reshape(bf16[2651904]{0:T(1024)(128)(2,1)} %slice.5204) | data formatting | bytes 10607616 | tf_op jit(solution)/shard_map/reshape | solution.py:38
  89.2 3.3 fusion.10
  92.5 1.9 convert_reduce_fusion
  94.5 0.9 fusion.14
  95.4 1.2 convolution_convert_fusion.1
  96.6 1.0 copy.14
  97.6 10.3 %all-to-all-start.1 = ((bf16[64,2,1152]{2,1,0:T(2,128)(2,1)}), bf16[64,2,1152]{2,1,0:T(2,128)(2,1)S(1)}, u32[]{:S(2)}, u32[]{:S(2)}) async-start(bf16[64,2,1152]{2,1,0:T(2,128)(2,1)} %copy.14), calls=%async_computation.1 | async-start | bytes 589824 | tf_op jit(solution)/shard_map/all_to_all | solution.py:83
  108.1 12.4 %all-to-all-done.1 = bf16[64,2,1152]{2,1,0:T(2,128)(2,1)S(1)} async-done(((bf16[64,2,1152]{2,1,0:T(2,128)(2,1)}), bf16[64,2,1152]{2,1,0:T(2,128)(2,1)S(1)}, u32[]{:S(2)}, u32[]{:S(2)}) %all-to-all-start.1) | async-done | bytes 294944 | tf_op jit(solution)/shard_map/all_to_all | solution.py:83
  120.9 0.6 stack.3228
  121.5 5.0 %all-to-all-start.2 = ((bf16[4,1,128,64]{2,3,1,0:T(8,128)(2,1)}), bf16[4,1,128,64]{2,3,1,0:T(8,128)(2,1)S(1)}, u32[]{:S(2)}, u32[]{:S(2)}) async-start(bf16[4,1,128,64]{2,3,1,0:T(8,128)(2,1)} %stack.3228), calls=%async_computation.2 | async-start | bytes 131072 | tf_op jit(solution)/shard_map/all_to_all | solution.py:101
  126.5 1.3 fusion.44
  148.1 0.7 constant_dynamic-update-slice_fusion.254
  148.8 1.1 constant_dynamic-update-slice_fusion.253
  149.8 0.6 constant_dynamic-update-slice_fusion.252
  150.5 0.6 constant_dynamic-update-slice_fusion.251
  152.4 0.6 constant_dynamic-update-slice_fusion.248
  154.2 0.6 constant_dynamic-update-slice_fusion.245
  154.9 0.6 constant_dynamic-update-slice_fusion.244
  155.5 0.6 constant_dynamic-update-slice_fusion.243
  157.4 0.6 constant_dynamic-update-slice_fusion.240
  159.2 0.6 constant_dynamic-update-slice_fusion.237
  159.9 0.6 constant_dynamic-update-slice_fusion.236
  162.4 0.6 constant_dynamic-update-slice_fusion.232
  294.8 0.6 constant_dynamic-update-slice_fusion.17
  296.6 0.6 constant_dynamic-update-slice_fusion.14
  305.9 5.0 %convolution_bitcast_fusion.1 = f32[1,128,64,128]{3,2,1,0:T(8,128)} fusion(bf16[128,128,128]{2,0,1:T(8,128)(2,1)} %copy-done.12, bf16[4,1,128,64]{2,3,1,0:T(8,128)(2,1)S(1)} %all-to-all-done.2), kind=kOutput, calls=%fused_computation.16 | convolution fusion | flops 268435456 | bytes 8404992 | tf_op jit(solution)/shard_map/tk,tjr->jkr/dot_general | solution.py:113
  310.9 2.8 convolution_bitcast_fusion.2
  313.7 0.8 copy-done.9
  314.4 2.8 convolution_bitcast_fusion.3
  317.2 0.8 copy-done.7
  318.0 2.8 convolution_bitcast_fusion.4
  320.7 0.8 copy-done.5
  321.5 2.8 convolution_bitcast_fusion.5
  324.3 0.8 copy-done.3
  325.0 2.9 convolution_bitcast_fusion.6
  327.9 4.9 %convolution_bitcast_fusion.7 = f32[1,128,64,128]{3,2,1,0:T(8,128)} fusion(bf16[128,128,128]{2,0,1:T(8,128)(2,1)} %constant_dynamic-update-slice_fusion.128, bf16[4,1,128,64]{2,3,1,0:T(8,128)(2,1)S(1)} %all-to-all-done.2), kind=kOutput, calls=%fused_computation.22 | convolution fusion | flops 268435456 | bytes 8404992 | tf_op jit(solution)/shard_map/tk,tjr->jkr/dot_general | solution.py:113
  332.7 4.9 %convolution_bitcast_fusion.8 = f32[1,128,64,128]{3,2,1,0:T(8,128)} fusion(bf16[128,128,128]{2,0,1:T(8,128)(2,1)} %constant_dynamic-update-slice_fusion, bf16[4,1,128,64]{2,3,1,0:T(8,128)(2,1)S(1)} %all-to-all-done.2), kind=kOutput, calls=%fused_computation.23 | convolution fusion | flops 268435456 | bytes 8404992 | tf_op jit(solution)/shard_map/tk,tjr->jkr/dot_general | solution.py:113
  337.7 16.4 %fusion.2 = f32[1,256,64,128]{3,2,1,0:T(8,128)} fusion(f32[1,128,64,128]{3,2,1,0:T(8,128)} %convolution_bitcast_fusion.7, f32[1,128,64,128]{3,2,1,0:T(8,128)} %convolution_bitcast_fusion.8, f32[1,128,64,128]{3,2,1,0:T(8,128)} %convolution_bitcast_fusion.5, f32[1,128,64,128]{3,2,1,0:T(8,128)} %convolution_bitcast_fusion.6, ...), kind=kLoop, calls=%fused_computation.5 | loop fusion | flops 16777216 | bytes 41975808 | tf_op jit(solution)/shard_map/mul | solution.py:122
  (1069 shorter events, 166.9 us)
Async XLA Ops:
  6.5 4.6 %copy-start = (bf16[64]{0:T(256)(128)(2,1)S(1)}, bf16[64]{0:T(256)(128)(2,1)}, u32[]{:S(2)}) copy-start(bf16[64]{0:T(256)(128)(2,1)} %param.7) | copy-start | bytes 388
  7.8 24.7 %collective-permute-start = (bf16[32,8192]{1,0:T(8,128)(2,1)S(1)}, bf16[32,8192]{1,0:T(8,128)(2,1)S(1)}, u32[]{:S(2)}, u32[]{:S(2)}) collective-permute-start(bf16[32,8192]{1,0:T(8,128)(2,1)S(1)} %get-tuple-element.5), channel_id=1, source_target_pairs={{0,4},{4,8},{8,12},{12,16},{16,20},{20,24},{24,28},{28,32},{32,36}... | collective-permute-start | bytes 1572872 | tf_op jit(solution)/shard_map/ppermute | solution.py:21
  9.6 23.0 %collective-permute-start.1 = (bf16[32,8192]{1,0:T(8,128)(2,1)S(1)}, bf16[32,8192]{1,0:T(8,128)(2,1)S(1)}, u32[]{:S(2)}, u32[]{:S(2)}) collective-permute-start(bf16[32,8192]{1,0:T(8,128)(2,1)S(1)} %get-tuple-element.6), channel_id=1, source_target_pairs={{4,0},{8,4},{12,8},{16,12},{20,16},{24,20},{28,24},{32,28},{36,32}... | collective-permute-start | bytes 1572872 | tf_op jit(solution)/shard_map/ppermute | solution.py:23
  32.6 19.8 %copy-start.14 = (bf16[255]{0:T(256)(128)(2,1)S(1)}, bf16[255]{0:T(256)(128)(2,1)}, u32[]{:S(2)}) copy-start(bf16[255]{0:T(256)(128)(2,1)} %param.8) | copy-start | bytes 1534
  36.0 53.1 %all-to-all-start = ((bf16[18,64,128]{2,0,1:T(8,128)(2,1)}), bf16[18,64,128]{2,0,1:T(8,128)(2,1)S(1)}, u32[]{:S(2)}, u32[]{:S(2)}) async-start(bf16[18,64,128]{2,0,1:T(8,128)(2,1)} %copy.12), calls=%async_computation | async-start | bytes 786432 | tf_op jit(solution)/shard_map/all_to_all | solution.py:61
  51.8 74.7 %all-gather.3.cloned.1.call-start = ((), (), s32[]{:S(2)}) async-start(), calls=%async_computation.3 | async-start | bytes 1474560 | tf_op jit(solution)/shard_map/all_gather | solution.py:99
  75.8 13.2 %copy-start.13 = (s32[64,64]{1,0:T(8,128)S(1)}, s32[64,64]{1,0:T(8,128)}, u32[]{:S(2)}) copy-start(s32[64,64]{1,0:T(8,128)} %param.9) | copy-start | bytes 49156
  89.0 19.0 %copy-start.15 = (s32[1,64]{1,0:T(1,128)S(1)}, s32[1,64]{1,0:T(1,128)}, u32[]{:S(2)}) copy-start(s32[1,64]{1,0:T(1,128)} %param.11) | copy-start | bytes 772
  89.0 19.0 %copy-start.16 = (s32[1,64]{1,0:T(1,128)S(1)}, s32[1,64]{1,0:T(1,128)}, u32[]{:S(2)}) copy-start(s32[1,64]{1,0:T(1,128)} %param.10) | copy-start | bytes 772
  97.6 22.9 %all-to-all-start.1 = ((bf16[64,2,1152]{2,1,0:T(2,128)(2,1)}), bf16[64,2,1152]{2,1,0:T(2,128)(2,1)S(1)}, u32[]{:S(2)}, u32[]{:S(2)}) async-start(bf16[64,2,1152]{2,1,0:T(2,128)(2,1)} %copy.14), calls=%async_computation.1 | async-start | bytes 589824 | tf_op jit(solution)/shard_map/all_to_all | solution.py:83
  121.5 184.4 %all-to-all-start.2 = ((bf16[4,1,128,64]{2,3,1,0:T(8,128)(2,1)}), bf16[4,1,128,64]{2,3,1,0:T(8,128)(2,1)S(1)}, u32[]{:S(2)}, u32[]{:S(2)}) async-start(bf16[4,1,128,64]{2,3,1,0:T(8,128)(2,1)} %stack.3228), calls=%async_computation.2 | async-start | bytes 131072 | tf_op jit(solution)/shard_map/all_to_all | solution.py:101
  132.3 3.1 copy-start.12
  135.3 3.1 copy-start.10
  138.4 3.1 copy-start.8
  141.5 3.5 copy-start.6
  145.0 4.9 %copy-start.4 = (bf16[128,128,128]{2,0,1:T(8,128)(2,1)}, bf16[128,128,128]{2,0,1:T(8,128)(2,1)S(1)}, u32[]{:S(2)}) copy-start(bf16[128,128,128]{2,0,1:T(8,128)(2,1)S(1)} %constant_dynamic-update-slice_fusion.384) | copy-start | bytes 12582916
  148.1 81.2 %copy-start.2 = (bf16[128,128,128]{2,0,1:T(8,128)(2,1)}, bf16[128,128,128]{2,0,1:T(8,128)(2,1)S(1)}, u32[]{:S(2)}) copy-start(bf16[128,128,128]{2,0,1:T(8,128)(2,1)S(1)} %constant_dynamic-update-slice_fusion.256) | copy-start | bytes 12582916
  305.9 5.0 %copy-start.11 = (bf16[128,128,128]{2,0,1:T(8,128)(2,1)S(1)}, bf16[128,128,128]{2,0,1:T(8,128)(2,1)}, u32[]{:S(2)}) copy-start(bf16[128,128,128]{2,0,1:T(8,128)(2,1)} %copy-done.10) | copy-start | bytes 12582916
  310.9 3.5 copy-start.9
  314.4 3.5 copy-start.7
  318.0 3.5 copy-start.5
  321.5 3.5 copy-start.3
  337.6 16.4 %copy-start.1 = (bf16[64]{0:T(256)(128)(2,1)S(1)}, bf16[64]{0:T(256)(128)(2,1)}, u32[]{:S(2)}) copy-start(bf16[64]{0:T(256)(128)(2,1)} %param.7) | copy-start | bytes 388
Sparse Core Ops, SparseCore 0:
  92.6 27.0 all-gather.2
